TPU v7x, 256 devices: a whole 4x4x8 slice. The times are simulated.
256 devices in a mesh: dp: 8 (over x, y_hi), row: 32 (over y_lo, z, core).
Axes of the slice: x: 4, y: 4 (y_hi: 2, y_lo: 2; y = y_hi * 2 + y_lo), z: 8, core: 2. Of those that a mesh axis runs over, the one named last changes fastest.
Arguments:
- patch_queries: bfloat16 [8, 4096, 512], P('dp', 'row'), may hold values from -6 to 6
- patch_keys: bfloat16 [8, 4096, 512], P('dp', 'row'), may hold values from -6 to 6
- scan_input: float32 [8, 4096, 512], P('dp', 'row'), may hold values from -6 to 6
- decay_rate: float32 [8, 4096, 512], P('dp', 'row'), may hold values from 0.4 to 1, as said below
- gate_logit: bfloat16 [8, 4096, 512], P('dp', 'row'), may hold values from -6 to 6
- grad_output: bfloat16 [8, 4096, 1024], P('dp', 'row'), may hold values from -6 to 6
- output_weight: bfloat16 [1024, 512], replicated, may hold values from -0.25 to 0.25
Outputs:
- grad_queries: bfloat16 [8, 4096, 512], P('dp', 'row')
- grad_keys: bfloat16 [8, 4096, 512], P('dp', 'row')
- grad_input: float32 [8, 4096, 512], P('dp', 'row')
- grad_decay: float32 [8, 4096, 512], P('dp', 'row')
- grad_gate: bfloat16 [8, 4096, 512], P('dp', 'row')
- grad_weight: float32 [1024, 512], P(('dp', 'row'))
Inputs may be any that keep to these rules, and one draw needn't show every extreme that they name: `decay_rate`: forget gates lie strictly below 1.
All inputs are finite; a program needn't handle non-finite values.
Results may differ from a plain program's by a relative error of at most 0.012.
The roundings to bfloat16 on the way count: a program that leaves them out, or rounds other values in their place, can miss the bound.
Values may be sent and summed in bfloat16 or wider, within the bound.
No kernel may reach another device: no remote copies, remote signals or barrier semaphores. Data moves between devices by JAX's collectives and lax.ppermute only.
A program may use at most 128 MiB of HBM per device.

v0:
```python
import jax
import jax.numpy as jnp
from jax import lax
from jax.sharding import PartitionSpec as P

HEADS = 8
HEAD_DIM = 64
lowest_start = -1e30


def prefix(x, axis, combine, identity, reverse):
    length, index = (lax.axis_size(axis), lax.axis_index(axis))
    everything = jax.tree.map(lambda part: lax.all_gather(part, axis), x)
    start = jax.tree.map(
        lambda part, zero: jnp.broadcast_to(jnp.asarray(zero, part.dtype), part.shape), x, identity
    )

    def hop(k, before):
        at = length - 1 - k if reverse else k
        reached = at > index if reverse else at < index
        new = combine(before, jax.tree.map(lambda part: part[at], everything))
        return jax.tree.map(lambda a, b: jnp.where(reached, a, b), new, before)

    return lax.fori_loop(0, length, hop, start)


def compose(earlier, later):
    return (later[0] * earlier[0], later[0] * earlier[1] + later[1])


def silu_slope(gate_float):
    sigmoid_value = jax.nn.sigmoid(gate_float)
    return sigmoid_value * (1.0 + gate_float * (1.0 - sigmoid_value))


def block_layout(length):
    block_rows = 512
    return (block_rows, length // block_rows)


def to_heads(array):
    return array.reshape(array.shape[0], array.shape[1], HEADS, HEAD_DIM)


def carry_states(totals):
    return prefix(
        totals, "row", compose, (jnp.ones_like(totals[0]), jnp.zeros_like(totals[1])), False
    )[1]


def carry_adjoints(totals):
    return prefix(
        totals, "row", compose, (jnp.ones_like(totals[0]), jnp.zeros_like(totals[1])), True
    )[1]


def body(patch_queries, patch_keys, scan_input, decay_rate, gate_logit, grad_output, output_weight):
    scaling = HEAD_DIM ** (-0.5)
    image_count, row_count, channels = patch_queries.shape
    local_gain, local_states = lax.associative_scan(compose, (decay_rate, scan_input), axis=1)
    incoming = carry_states((local_gain[:, -1], local_states[:, -1]))
    states = local_states + local_gain * incoming[:, None]
    gate_float = gate_logit.astype(jnp.float32)
    activation = jax.nn.silu(gate_float)
    value_low = (states * activation).astype(jnp.bfloat16)
    grad_attended = jnp.einsum(
        "btd,dc->btc", grad_output, output_weight, preferred_element_type=jnp.float32
    ).astype(jnp.bfloat16)
    query_heads = to_heads(patch_queries)
    grad_heads = to_heads(grad_attended)
    key_heads = to_heads(patch_keys)
    value_heads = to_heads(value_low)
    start_top = jnp.full((image_count, HEADS, row_count), lowest_start, jnp.float32)
    zero_totals = jnp.zeros((image_count, HEADS, row_count), jnp.float32)
    zero_heads = jnp.zeros((image_count, row_count, HEADS, HEAD_DIM), jnp.float32)
    portion = lax.all_gather(patch_keys, "row", axis=1, tiled=True)
    block_rows, count_blocks = block_layout(portion.shape[1])

    def softmax_one_block(block_index, running):
        key_block = to_heads(
            lax.dynamic_slice_in_dim(portion, block_index * block_rows, block_rows, 1)
        )
        scores = (
            jnp.einsum(
                "bthd,bjhd->bhtj", query_heads, key_block, preferred_element_type=jnp.float32
            )
            * scaling
        )
        new_top = jnp.maximum(running[0], jnp.max(scores, axis=-1))
        new_sum = running[1] * jnp.exp(running[0] - new_top) + jnp.sum(
            jnp.exp(scores - new_top[..., None]), axis=-1
        )
        return (new_top, new_sum)

    running_top, total_sum = lax.fori_loop(
        0, count_blocks, softmax_one_block, (start_top, zero_totals)
    )
    log_total = running_top + jnp.log(total_sum)
    key_portion = lax.all_gather(patch_keys, "row", axis=1, tiled=True)
    value_portion = lax.all_gather(value_low, "row", axis=1, tiled=True)
    query_block_rows, count_blocks = block_layout(key_portion.shape[1])

    def query_one_block(block_index, running):
        attended_sum, row_delta, first_sum, second_sum = running
        key_block = to_heads(
            lax.dynamic_slice_in_dim(
                key_portion, block_index * query_block_rows, query_block_rows, 1
            )
        )
        value_block = to_heads(
            lax.dynamic_slice_in_dim(
                value_portion, block_index * query_block_rows, query_block_rows, 1
            )
        )
        scores = (
            jnp.einsum(
                "bthd,bjhd->bhtj", query_heads, key_block, preferred_element_type=jnp.float32
            )
            * scaling
        )
        weights = jnp.exp(scores - log_total[..., None])
        weights_low = weights.astype(jnp.bfloat16)
        grad_weights = jnp.einsum(
            "bthd,bjhd->bhtj", grad_heads, value_block, preferred_element_type=jnp.float32
        )
        row_delta = row_delta + jnp.sum(weights * grad_weights, axis=-1)
        weighted = (weights * grad_weights).astype(jnp.bfloat16)
        attended_sum = attended_sum + jnp.einsum(
            "bhtj,bjhd->bthd", weights_low, value_block, preferred_element_type=jnp.float32
        )
        first_sum = first_sum + jnp.einsum(
            "bhtj,bjhd->bthd", weighted, key_block, preferred_element_type=jnp.float32
        )
        second_sum = second_sum + jnp.einsum(
            "bhtj,bjhd->bthd", weights_low, key_block, preferred_element_type=jnp.float32
        )
        return (attended_sum, row_delta, first_sum, second_sum)

    folded = lax.fori_loop(
        0, count_blocks, query_one_block, (zero_heads, zero_totals, zero_heads, zero_heads)
    )
    attended_sum, row_delta, first_sum, second_sum = folded
    attended = attended_sum.astype(jnp.bfloat16).reshape(image_count, row_count, channels)
    delta_rows = jnp.transpose(row_delta, (0, 2, 1))[..., None]
    grad_queries = (
        ((first_sum - delta_rows * second_sum) * scaling)
        .astype(jnp.bfloat16)
        .reshape(image_count, row_count, channels)
    )
    all_totals, all_deltas = (
        lax.all_gather(jnp.transpose(log_total, (0, 2, 1)), "row", axis=1, tiled=True),
        lax.all_gather(jnp.transpose(row_delta, (0, 2, 1)), "row", axis=1, tiled=True),
    )
    query_portion = lax.all_gather(patch_queries, "row", axis=1, tiled=True)
    grad_portion = lax.all_gather(grad_attended, "row", axis=1, tiled=True)
    key_block_rows, count_blocks = block_layout(query_portion.shape[1])

    def key_one_block(block_index, running):
        key_sum, value_sum = running
        offset = block_index * key_block_rows
        query_block = to_heads(lax.dynamic_slice_in_dim(query_portion, offset, key_block_rows, 1))
        grad_block = to_heads(lax.dynamic_slice_in_dim(grad_portion, offset, key_block_rows, 1))
        total_block = jnp.transpose(
            lax.dynamic_slice_in_dim(all_totals, offset, key_block_rows, 1), (0, 2, 1)
        )
        delta_block = jnp.transpose(
            lax.dynamic_slice_in_dim(all_deltas, offset, key_block_rows, 1), (0, 2, 1)
        )
        scores = (
            jnp.einsum(
                "bthd,bjhd->bhtj", query_block, key_heads, preferred_element_type=jnp.float32
            )
            * scaling
        )
        weights = jnp.exp(scores - total_block[..., None])
        grad_weights = jnp.einsum(
            "bthd,bjhd->bhtj", grad_block, value_heads, preferred_element_type=jnp.float32
        )
        grad_scores = (weights * (grad_weights - delta_block[..., None])).astype(jnp.bfloat16)
        key_sum = key_sum + jnp.einsum(
            "bhtj,bthd->bjhd", grad_scores, query_block, preferred_element_type=jnp.float32
        )
        value_sum = value_sum + jnp.einsum(
            "bhtj,bthd->bjhd",
            weights.astype(jnp.bfloat16),
            grad_block,
            preferred_element_type=jnp.float32,
        )
        return (key_sum, value_sum)

    key_sum, value_sum = lax.fori_loop(0, count_blocks, key_one_block, (zero_heads, zero_heads))
    grad_keys = (key_sum * scaling).astype(jnp.bfloat16).reshape(image_count, row_count, channels)
    value_gradient = value_sum.reshape(image_count, row_count, channels)
    grad_gate = (value_gradient * states * silu_slope(gate_float)).astype(jnp.bfloat16)
    shifted = jnp.concatenate([decay_rate[:, 1:], jnp.ones_like(decay_rate[:, :1])], axis=1)
    tail_gain, local_adjoint = lax.associative_scan(
        compose, (shifted, value_gradient * activation), reverse=True, axis=1
    )
    head_rate = decay_rate[:, 0]
    arriving = carry_adjoints((head_rate * tail_gain[:, 0], head_rate * local_adjoint[:, 0]))
    grad_input = local_adjoint + tail_gain * arriving[:, None]
    earlier = jnp.concatenate([incoming[:, None], states[:, :-1]], axis=1)
    grad_decay = grad_input * earlier
    grad_weight = lax.psum_scatter(
        jnp.einsum("btd,btc->dc", grad_output, attended, preferred_element_type=jnp.float32),
        ("dp", "row"),
        scatter_dimension=0,
        tiled=True,
    )
    return (grad_queries, grad_keys, grad_input, grad_decay, grad_gate, grad_weight)


def solution(mesh):
    in_specs = (
        P("dp", "row", None),
        P("dp", "row", None),
        P("dp", "row", None),
        P("dp", "row", None),
        P("dp", "row", None),
        P("dp", "row", None),
        P(),
    )
    out_specs = (
        P("dp", "row", None),
        P("dp", "row", None),
        P("dp", "row", None),
        P("dp", "row", None),
        P("dp", "row", None),
        P(("dp", "row"), None),
    )
    return jax.shard_map(body, mesh=mesh, in_specs=in_specs, out_specs=out_specs, check_vma=False)
```

profile of v0, /device:TPU:2, one launch (start us, length us, event | category | flops | bytes accessed | tf_op | source)
XLA Modules:
  0.0 1026.0 jit_solution(15914821030163046469)
XLA Ops:
  13.7 3.7 slice.487
  17.4 3.3 slice.449
  20.7 3.7 slice.446
  24.5 3.3 slice.447
  27.8 3.2 slice.448
  31.0 3.2 slice.451
  94.5 2.7 pad.177
  116.7 2.7 pad.193
  121.2 2.7 pad.192
  153.4 4.8 pad.201
  167.0 4.3 pad.200
  171.6 4.6 pad.187
  176.5 4.3 pad.186
  181.1 37.3 %all_gather.33 = f32[32,1,512]{2,1,0:T(1,128)S(1)} all-gather(f32[1,1,512]{2,1,0:T(1,128)S(1)} %copy.196), channel_id=1, replica_groups=mesh['dp'=8,'row'=32] {'row'}, dimensions={0}, use_global_device_ids=true | all-gather | bytes 67584 | tf_op jit(solution)/shard_map/all_gather | solution.py:13
  218.5 30.8 %all_gather.34 = f32[32,1,512]{2,1,0:T(1,128)S(1)} all-gather(f32[1,1,512]{2,1,0:T(1,128)S(1)} %copy.197), channel_id=1, replica_groups=mesh['dp'=8,'row'=32] {'row'}, dimensions={0}, use_global_device_ids=true | all-gather | bytes 67584 | tf_op jit(solution)/shard_map/all_gather | solution.py:13
  255.4 6.0 slice.507
  261.5 6.0 slice.509
  267.5 6.4 slice.516
  279.5 16.3 %while.83 = (s32[]{:T(128)}, f32[1,8,128]{2,1,0:T(8,128)S(1)}, f32[1,8,128]{2,1,0:T(8,128)S(1)}, bf16[1,4096,512]{1,2,0:T(8,128)(2,1)}, bf16[1,128,8,64]{1,3,2,0...) while((s32[]{:T(128)}, f32[1,8,128]{2,1,0:T(8,128)S(1)}, ...), condition=%wide.region_5.6_spmd.clone, body=%wide.region_2.5_spmd.clone.sunk | while | flops 69735432 | bytes 5951650 | solution.py:95
  295.8 35.0 %all_gather.38 = f32[1,4096,8]{1,2,0:T(8,128)} all-gather(f32[1,128,8]{1,2,0:T(8,128)S(1)} %bitcast.269), channel_id=1, replica_groups=mesh['dp'=8,'row'=32] {'row'}, dimensions={1}, use_global_device_ids=true | all-gather | bytes 135168 | tf_op jit(solution)/shard_map/all_gather | solution.py:151
  330.9 56.9 %while.84 = (s32[]{:T(128)}, f32[1,128,8,64]{1,3,2,0:T(8,128)}, f32[1,8,128]{2,1,0:T(8,128)S(1)}, f32[1,128,8,64]{1,3,2,0:T(8,128)S(1)}, f32[1,128,8,64]{1,3,2,0...) while((s32[]{:T(128)}, f32[1,128,8,64]{1,3,2,0:T(8,128)}, ...), condition=%wide.region_8.9_spmd.clone, body=%wide.region_6.8_spmd.clone.sunk | while | flops 341705728 | bytes 17592552 | solution.py:139
  387.8 33.9 %all_gather.40 = f32[1,4096,8]{1,2,0:T(8,128)} all-gather(f32[1,128,8]{1,2,0:T(8,128)S(1)} %bitcast.277), channel_id=1, replica_groups=mesh['dp'=8,'row'=32] {'row'}, dimensions={1}, use_global_device_ids=true | all-gather | bytes 135168 | tf_op jit(solution)/shard_map/all_gather | solution.py:152
  421.6 40.4 %all-gather.12.cloned.1.call-done = bf16[4096,512]{1,0:T(8,128)(2,1)} async-done(((bf16[128,512]{1,0:T(8,128)(2,1)}), bf16[4096,512]{1,0:T(8,128)(2,1)}) %all-gather.12.cloned.1.call-update) | async-done | bytes 4194320 | tf_op jit(solution)/shard_map/all_gather | solution.py:155
  462.0 85.3 %while.85 = (s32[]{:T(128)}, f32[1,128,8,64]{1,3,2,0:T(8,128)}, f32[1,128,8,64]{1,3,2,0:T(8,128)}, bf16[1,4096,512]{1,2,0:T(8,128)(2,1)}, bf16[1,128,8,64]{1,3,2...) while((s32[]{:T(128)}, f32[1,128,8,64]{1,3,2,0:T(8,128)}, ...), condition=%wide.region_10.11_spmd.clone, body=%wide.region_9.10_spmd.clone.sunk | while | flops 272891904 | bytes 15057126 | solution.py:191
  466.9 3.4 fusion.117
  476.7 3.5 fusion.117
  487.5 3.5 fusion.117
  498.2 3.5 fusion.117
  509.0 3.5 fusion.117
  519.7 3.5 fusion.117
  530.5 3.5 fusion.117
  541.2 3.5 fusion.117
  548.6 6.0 slice.513
  554.6 6.4 slice.511
  561.9 3.3 slice.519
  565.2 3.2 slice.523
  568.4 3.3 slice.521
  571.7 3.2 slice.520
  618.3 3.7 slice.518
  622.0 3.7 slice.559
  625.7 6.7 slice.561
  672.7 4.3 pad.214
  677.0 4.4 pad.215
  681.6 4.6 pad.228
  686.2 4.4 pad.229
  691.0 32.0 %all_gather.41 = f32[32,1,512]{2,1,0:T(1,128)S(1)} all-gather(f32[1,1,512]{2,1,0:T(1,128)S(1)} %copy.218), channel_id=1, replica_groups=mesh['dp'=8,'row'=32] {'row'}, dimensions={0}, use_global_device_ids=true | all-gather | bytes 67584 | tf_op jit(solution)/shard_map/all_gather | solution.py:13
  723.1 31.0 %all_gather.42 = f32[32,1,512]{2,1,0:T(1,128)S(1)} all-gather(f32[1,1,512]{2,1,0:T(1,128)S(1)} %copy.219), channel_id=1, replica_groups=mesh['dp'=8,'row'=32] {'row'}, dimensions={0}, use_global_device_ids=true | all-gather | bytes 67584 | tf_op jit(solution)/shard_map/all_gather | solution.py:13
  763.6 253.6 %all-reduce.61.cloned.1.call-done = f32[1024,512]{0,1:T(8,128)} async-done(((f32[1024,512]{0,1:T(8,128)}), f32[1024,512]{0,1:T(8,128)}) %all-reduce.61.cloned.1.call-update) | async-done | bytes 2097168
  (584 shorter events, 366.0 us)
Async XLA Ops:
  7.2 245.3 %copy-start = (bf16[1024,512]{1,0:T(8,128)(2,1)S(1)}, bf16[1024,512]{1,0:T(8,128)(2,1)}, u32[]{:S(2)}) copy-start(bf16[1024,512]{1,0:T(8,128)(2,1)} %param.23) | copy-start | bytes 3145732
  7.2 272.3 %all-gather.8.cloned.1.call-start = ((), (), s32[]{:S(2)}) async-start(), calls=%async_computation.1 | async-start | bytes 4325376 | tf_op jit(solution)/shard_map/all_gather | solution.py:99
  9.0 321.9 %all-gather.6.cloned.1.call-start = ((), (), s32[]{:S(2)}) async-start(), calls=%async_computation | async-start | bytes 4325376 | tf_op jit(solution)/shard_map/all_gather | solution.py:100
  72.9 12.6 %copy-start.12 = (f32[1,128,512]{2,1,0:T(8,128)S(1)}, f32[1,128,512]{2,1,0:T(8,128)}, u32[]{:S(2)}) copy-start(f32[1,128,512]{2,1,0:T(8,128)} %param.20) | copy-start | bytes 786436
  89.2 161.4 %copy-start.14 = (bf16[1,128,512]{1,2,0:T(8,128)(2,1)}, bf16[1,128,512]{1,2,0:T(8,128)(2,1)S(1)}, u32[]{:S(2)}) copy-start(bf16[1,128,512]{1,2,0:T(8,128)(2,1)S(1)} %copy.198) | copy-start | bytes 393220
  94.5 2.7 copy-start.7
  121.2 5.2 copy-start.8
  141.6 5.5 copy-start.29
  148.8 14.4 %copy-start.27 = (f32[1,31,512]{1,2,0:T(8,128)S(1)}, f32[1,31,512]{1,2,0:T(8,128)}, u32[]{:S(2)}) copy-start(f32[1,31,512]{1,2,0:T(8,128)} %get-tuple-element.1003) | copy-start | bytes 190468
  153.3 12.2 %copy-start.35 = (f32[1,1,512]{2,1,0:T(1,128)S(1)}, f32[1,1,512]{2,1,0:T(1,128)}, u32[]{:S(2)}) copy-start(f32[1,1,512]{2,1,0:T(1,128)} %slice.490) | copy-start | bytes 6148
  165.7 5.6 copy-start.9
  165.7 10.5 %copy-start.34 = (f32[1,1,512]{2,1,0:T(1,128)S(1)}, f32[1,1,512]{2,1,0:T(1,128)}, u32[]{:S(2)}) copy-start(f32[1,1,512]{2,1,0:T(1,128)} %slice.439) | copy-start | bytes 6148
  176.3 75.3 %copy-start.32 = (bf16[1,128,512]{2,1,0:T(8,128)(2,1)S(1)}, bf16[1,128,512]{2,1,0:T(8,128)(2,1)}, u32[]{:S(2)}) copy-start(bf16[1,128,512]{2,1,0:T(8,128)(2,1)} %param.17) | copy-start | bytes 393220
  176.5 76.0 %copy-start.20 = (bf16[1,128,1024]{2,1,0:T(8,128)(2,1)S(1)}, bf16[1,128,1024]{2,1,0:T(8,128)(2,1)}, u32[]{:S(2)}) copy-start(bf16[1,128,1024]{2,1,0:T(8,128)(2,1)} %param.22) | copy-start | bytes 786436
  249.3 5.9 copy-start.13
  251.6 170.1 %all-gather.10.cloned.1.call-start = ((), (), s32[]{:S(2)}) async-start(), calls=%async_computation.2 | async-start | bytes 4325376 | tf_op jit(solution)/shard_map/all_gather | solution.py:154
  252.4 209.6 %all-gather.12.cloned.1.call-start = ((), (), s32[]{:S(2)}) async-start(), calls=%async_computation.3 | async-start | bytes 4325376 | tf_op jit(solution)/shard_map/all_gather | solution.py:155
  253.5 763.7 %all-reduce.61.cloned.1.call-start = ((), (), s32[]{:S(2)}) async-start(), calls=%async_computation.4 | async-start | bytes 4194304
  255.4 24.1 %copy-start.3 = (bf16[1,128,512]{1,2,0:T(8,128)(2,1)S(1)}, bf16[1,128,512]{1,2,0:T(8,128)(2,1)}, u32[]{:S(2)}) copy-start(bf16[1,128,512]{1,2,0:T(8,128)(2,1)} %copy.200) | copy-start | bytes 393220
  338.1 2.3 copy-start.6
  345.4 2.2 copy-start.6
  352.8 2.2 copy-start.6
  360.1 2.2 copy-start.6
  367.5 2.3 copy-start.6
  374.9 2.2 copy-start.6
  382.2 2.2 copy-start.6
  473.1 1.6 copy-start.2
  494.6 1.6 copy-start.2
  537.6 1.6 copy-start.2
  547.3 14.5 %copy-start.25 = (f32[1,64,512]{1,2,0:T(8,128)S(1)}, f32[1,64,512]{1,2,0:T(8,128)}, u32[]{:S(2)}) copy-start(f32[1,64,512]{1,2,0:T(8,128)} %slice.510) | copy-start | bytes 393220
  547.3 14.5 %copy-start.26 = (f32[1,64,512]{1,2,0:T(8,128)S(1)}, f32[1,64,512]{1,2,0:T(8,128)}, u32[]{:S(2)}) copy-start(f32[1,64,512]{1,2,0:T(8,128)} %slice.517) | copy-start | bytes 393220
  610.6 22.6 %copy-start.17 = (f32[1,2,512]{1,2,0:T(8,128)S(1)}, f32[1,2,512]{1,2,0:T(8,128)}, u32[]{:S(2)}) copy-start(f32[1,2,512]{1,2,0:T(8,128)} %pad_add_fusion) | copy-start | bytes 12292
  612.5 21.0 %copy-start.15 = (f32[1,1,512]{1,2,0:T(8,128)S(1)}, f32[1,1,512]{1,2,0:T(8,128)}, u32[]{:S(2)}) copy-start(f32[1,1,512]{1,2,0:T(8,128)} %get-tuple-element.980) | copy-start | bytes 6148
  612.5 21.0 %copy-start.16 = (f32[1,1,512]{1,2,0:T(8,128)S(1)}, f32[1,1,512]{1,2,0:T(8,128)}, u32[]{:S(2)}) copy-start(f32[1,1,512]{1,2,0:T(8,128)} %get-tuple-element.981) | copy-start | bytes 6148
  643.3 2.4 copy-start.18
  651.3 3.3 copy-start.23
  659.1 4.7 copy-start.30
  663.8 3.6 copy-start.22
  667.4 5.0 copy-start.28
  670.2 2.4 copy-start.19
  672.5 18.0 %copy-start.10 = (f32[1,1,512]{1,2,0:T(8,128)S(1)}, f32[1,1,512]{1,2,0:T(8,128)}, u32[]{:S(2)}) copy-start(f32[1,1,512]{1,2,0:T(8,128)} %copy-done.9) | copy-start | bytes 6148
  681.4 72.7 %copy-start.4 = (f32[1,128,8,64]{1,3,2,0:T(8,128)S(1)}, f32[1,128,8,64]{1,3,2,0:T(8,128)}, u32[]{:S(2)}) copy-start(f32[1,128,8,64]{1,3,2,0:T(8,128)} %get-tuple-element.663) | copy-start | bytes 786436
  681.6 72.6 %copy-start.21 = (bf16[1,128,1024]{2,1,0:T(8,128)(2,1)S(1)}, bf16[1,128,1024]{2,1,0:T(8,128)(2,1)}, u32[]{:S(2)}) copy-start(bf16[1,128,1024]{2,1,0:T(8,128)(2,1)} %param.22) | copy-start | bytes 786436
  754.2 1.8 copy-start.33
  756.0 3.5 copy-start.31
  757.5 3.4 copy-start.11
  757.5 3.4 copy-start.24
  760.2 258.8 %copy-start.1 = (bf16[1024,512]{1,0:T(8,128)(2,1)S(1)}, bf16[1024,512]{1,0:T(8,128)(2,1)}, u32[]{:S(2)}) copy-start(bf16[1024,512]{1,0:T(8,128)(2,1)} %param.23) | copy-start | bytes 3145732
  (7 other events, 10.7 us)
Sparse Core Ops, SparseCore 0:
  10.3 75.1 all-gather.7
  251.7 69.4 all-gather.5
  323.6 71.0 all-gather.9
  396.4 65.5 all-gather.11
  756.1 261.0 all-reduce.60
where the time goes:
time: 1040 us; the launch traced here: 1030 us
  local copies, waits for them, and re-layouts  344 us (33%)
  waiting for transfers between devices  294 us (28%)
  blocking collectives  200 us (19%)
  matrix products  113 us (11%)
  other arithmetic  56 us (5%)
  between operations  15.7 us (2%)
    unnamed x6, waiting for transfers between devices  254 us
    all_gather x4, blocking collectives, prefix(): everything = jax.tree.map(lambda part: lax.all_gather(part, axis), x)  131 us
    slice x42, local copies, waits for them, and re-layouts, body(): lax.associative_scan(compose, (shifted, value_gradient * activation), rev...  101 us
    slice x37, local copies, waits for them, and re-layouts, body(): lax.associative_scan(compose, (decay_rate, scan_input), axis=1)  70.4 us
    pad x24, local copies, waits for them, and re-layouts, body(): lax.associative_scan(compose, (decay_rate, scan_input), axis=1)  54.1 us
    all_gather x1, waiting for transfers between devices, body(): grad_portion = lax.all_gather(grad_attended, 'row', axis=1, tiled=True)  40.4 us
    pad x24, local copies, waits for them, and re-layouts, body(): lax.associative_scan(compose, (shifted, value_gradient * activation), rev...  39.2 us
    all_gather x1, blocking collectives, body(): lax.all_gather(jnp.transpose(log_total, (0, 2, 1)), 'row', axis=1, tiled=...  35 us
  transfers between devices with their start and end apart: 5, of which 2 were waited for; matrix products, arithmetic and copies ran while one was open for 27% of the time, Pallas kernels for 0%

commit v1 on v0

--- a/solution.py
+++ b/solution.py
@@ -148,7 +148,15 @@
         .reshape(image_count, row_count, channels)
     )
     all_totals, all_deltas = (
-        lax.all_gather(jnp.transpose(log_total, (0, 2, 1)), "row", axis=1, tiled=True),
+        jnp.concatenate(
+            lax.all_to_all(
+                jnp.stack(lax.axis_size("row") * [jnp.transpose(log_total, (0, 2, 1))], axis=0),
+                axis_name="row",
+                split_axis=0,
+                concat_axis=0,
+            ),
+            axis=1,
+        ),
         lax.all_gather(jnp.transpose(row_delta, (0, 2, 1)), "row", axis=1, tiled=True),
     )
     query_portion = lax.all_gather(patch_queries, "row", axis=1, tiled=True)

time: 1040 us -> 759 us (0.73)
  waiting for transfers between devices: 294 us -> 61.1 us
  blocking collectives: 200 us -> 169 us
  matrix products: 113 us -> 97.4 us
    unnamed x6, waiting for transfers between devices: 254 us -> 0.08 us
    all_gather x1 -> x0, blocking collectives: 35 us -> none  [body(): lax.all_gather(jnp.transpose(log_total, (0, 2, 1)), 'row', axis=1, tiled=...]
    all_gather x1, waiting for transfers between devices: 0.01 us -> 25 us  [body(): value_portion = lax.all_gather(value_low, 'row', axis=1, tiled=True)]
    unnamed x98 -> x96, local copies, waits for them, and re-layouts: 21.7 us -> 21.7 us
  transfers between devices with their start and end apart: 5 -> 6, of which waited for: 2 -> 2; matrix products, arithmetic and copies ran while one was open for 27% -> 65% of each run, Pallas kernels for 0% -> 0%
where the time goes in v1:
time: 759 us; the launch traced here: 744 us
  local copies, waits for them, and re-layouts  340 us (45%)
  blocking collectives  169 us (22%)
  matrix products  97.4 us (13%)
  waiting for transfers between devices  61.1 us (8%)
  other arithmetic  52.5 us (7%)
  between operations  15.8 us (2%)
    all_gather x4, blocking collectives, prefix(): everything = jax.tree.map(lambda part: lax.all_gather(part, axis), x)  131 us
    slice x42, local copies, waits for them, and re-layouts, body(): lax.associative_scan(compose, (shifted, value_gradient * activation), rev...  98.7 us
    slice x37, local copies, waits for them, and re-layouts, body(): lax.associative_scan(compose, (decay_rate, scan_input), axis=1)  70.3 us
    pad x24, local copies, waits for them, and re-layouts, body(): lax.associative_scan(compose, (decay_rate, scan_input), axis=1)  54.1 us
    pad x24, local copies, waits for them, and re-layouts, body(): lax.associative_scan(compose, (shifted, value_gradient * activation), rev...  37.3 us
    all_gather x1, blocking collectives, body(): lax.all_gather(jnp.transpose(row_delta, (0, 2, 1)), 'row', axis=1, tiled=...  37.2 us
    all_gather x1, waiting for transfers between devices, body(): grad_portion = lax.all_gather(grad_attended, 'row', axis=1, tiled=True)  36 us
    dot_general x8, matrix products, key_one_block(): jnp.einsum('bhtj,bthd->bjhd', grad_scores, query_block, preferred_element...  27.8 us
  transfers between devices with their start and end apart: 6, of which 2 were waited for; matrix products, arithmetic and copies ran while one was open for 65% of the time, Pallas kernels for 0%

profile of v1, /device:TPU:2, one launch (start us, length us, event | category | flops | bytes accessed | tf_op | source)
XLA Modules:
  0.0 744.4 jit_solution(4293749214183398418)
XLA Ops:
  13.7 3.7 slice.487
  17.4 3.3 slice.449
  20.7 3.7 slice.446
  24.5 3.3 slice.447
  27.8 3.2 slice.448
  31.0 3.2 slice.451
  116.6 2.7 pad.193
  121.1 2.7 pad.192
  153.3 4.8 pad.201
  166.9 4.3 pad.200
  171.6 4.6 pad.187
  176.4 4.3 pad.186
  181.1 37.4 %all_gather.30 = f32[32,1,512]{2,1,0:T(1,128)S(1)} all-gather(f32[1,1,512]{2,1,0:T(1,128)S(1)} %copy.196), channel_id=1, replica_groups=mesh['dp'=8,'row'=32] {'row'}, dimensions={0}, use_global_device_ids=true | all-gather | bytes 67584 | tf_op jit(solution)/shard_map/all_gather | solution.py:13
  218.5 30.8 %all_gather.31 = f32[32,1,512]{2,1,0:T(1,128)S(1)} all-gather(f32[1,1,512]{2,1,0:T(1,128)S(1)} %copy.197), channel_id=1, replica_groups=mesh['dp'=8,'row'=32] {'row'}, dimensions={0}, use_global_device_ids=true | all-gather | bytes 67584 | tf_op jit(solution)/shard_map/all_gather | solution.py:13
  255.4 6.0 slice.507
  261.4 6.0 slice.509
  267.5 6.4 slice.516
  279.3 16.3 %while.83 = (s32[]{:T(128)}, f32[1,8,128]{2,1,0:T(8,128)S(1)}, f32[1,8,128]{2,1,0:T(8,128)S(1)}, bf16[1,4096,512]{1,2,0:T(8,128)(2,1)}, bf16[1,128,8,64]{1,3,2,0...) while((s32[]{:T(128)}, f32[1,8,128]{2,1,0:T(8,128)S(1)}, ...), condition=%wide.region_5.6_spmd.clone, body=%wide.region_2.5_spmd.clone.sunk | while | flops 69735432 | bytes 5951650 | solution.py:95
  295.6 25.0 %all-gather.6.cloned.1.call-done = bf16[1,4096,512]{1,2,0:T(8,128)(2,1)} async-done(((bf16[1,128,512]{1,2,0:T(8,128)(2,1)}), bf16[1,4096,512]{1,2,0:T(8,128)(2,1)}) %all-gather.6.cloned.1.call-update) | async-done | bytes 4194320 | tf_op jit(solution)/shard_map/all_gather | solution.py:100
  320.7 56.9 %while.84 = (s32[]{:T(128)}, f32[1,128,8,64]{1,3,2,0:T(8,128)}, f32[1,8,128]{2,1,0:T(8,128)S(1)}, f32[1,128,8,64]{1,3,2,0:T(8,128)S(1)}, f32[1,128,8,64]{1,3,2,0...) while((s32[]{:T(128)}, f32[1,128,8,64]{1,3,2,0:T(8,128)}, ...), condition=%wide.region_8.9_spmd.clone, body=%wide.region_6.8_spmd.clone.sunk | while | flops 341705728 | bytes 17592552 | solution.py:139
  380.0 5.9 all-to-all-start
  387.0 2.8 convolution_bitcast_fusion.4
  389.8 37.2 %all_gather.36 = f32[1,4096,8]{1,2,0:T(8,128)} all-gather(f32[1,128,8]{1,2,0:T(8,128)S(1)} %bitcast.281), channel_id=1, replica_groups=mesh['dp'=8,'row'=32] {'row'}, dimensions={1}, use_global_device_ids=true | all-gather | bytes 135168 | tf_op jit(solution)/shard_map/all_gather | solution.py:160
  427.0 36.0 %all-gather.12.cloned.1.call-done = bf16[4096,512]{1,0:T(8,128)(2,1)} async-done(((bf16[128,512]{1,0:T(8,128)(2,1)}), bf16[4096,512]{1,0:T(8,128)(2,1)}) %all-gather.12.cloned.1.call-update) | async-done | bytes 4194320 | tf_op jit(solution)/shard_map/all_gather | solution.py:163
  463.0 71.2 %while.85 = (s32[]{:T(128)}, f32[1,128,8,64]{1,3,2,0:T(8,128)}, f32[1,128,8,64]{1,3,2,0:T(8,128)S(1)}, bf16[1,4096,512]{1,2,0:T(8,128)(2,1)}, bf16[1,128,8,64]{1...) while((s32[]{:T(128)}, f32[1,128,8,64]{1,3,2,0:T(8,128)}, ...), condition=%wide.region_10.11_spmd.clone, body=%wide.region_9.10_spmd.clone.sunk | while | flops 272891904 | bytes 15057126 | solution.py:199
  467.2 3.4 fusion.117
  476.0 3.5 fusion.117
  484.9 3.5 fusion.117
  493.8 3.5 fusion.117
  502.7 3.5 fusion.117
  511.5 3.5 fusion.117
  520.4 3.5 fusion.117
  529.3 3.5 fusion.117
  535.5 6.0 slice.513
  541.5 6.4 slice.511
  548.8 3.3 slice.519
  552.1 3.2 slice.523
  555.3 3.3 slice.521
  558.6 3.2 slice.520
  601.3 3.7 slice.518
  605.0 3.7 slice.559
  608.7 6.7 slice.561
  648.1 4.3 pad.214
  652.5 4.4 pad.215
  657.0 4.6 pad.228
  661.6 4.4 pad.229
  666.4 32.4 %all_gather.37 = f32[32,1,512]{2,1,0:T(1,128)S(1)} all-gather(f32[1,1,512]{2,1,0:T(1,128)S(1)} %copy.218), channel_id=1, replica_groups=mesh['dp'=8,'row'=32] {'row'}, dimensions={0}, use_global_device_ids=true | all-gather | bytes 67584 | tf_op jit(solution)/shard_map/all_gather | solution.py:13
  699.0 30.9 %all_gather.38 = f32[32,1,512]{2,1,0:T(1,128)S(1)} all-gather(f32[1,1,512]{2,1,0:T(1,128)S(1)} %copy.219), channel_id=1, replica_groups=mesh['dp'=8,'row'=32] {'row'}, dimensions={0}, use_global_device_ids=true | all-gather | bytes 67584 | tf_op jit(solution)/shard_map/all_gather | solution.py:13
  (584 shorter events, 342.5 us)
Async XLA Ops:
  7.2 245.3 %copy-start = (bf16[1024,512]{1,0:T(8,128)(2,1)S(1)}, bf16[1024,512]{1,0:T(8,128)(2,1)}, u32[]{:S(2)}) copy-start(bf16[1024,512]{1,0:T(8,128)(2,1)} %param.23) | copy-start | bytes 3145732
  7.2 272.2 %all-gather.8.cloned.1.call-start = ((), (), s32[]{:S(2)}) async-start(), calls=%async_computation.2 | async-start | bytes 4325376 | tf_op jit(solution)/shard_map/all_gather | solution.py:99
  9.0 311.7 %all-gather.6.cloned.1.call-start = ((), (), s32[]{:S(2)}) async-start(), calls=%async_computation.1 | async-start | bytes 4325376 | tf_op jit(solution)/shard_map/all_gather | solution.py:100
  69.9 1.5 copy-start.5
  72.9 12.6 %copy-start.13 = (f32[1,128,512]{2,1,0:T(8,128)S(1)}, f32[1,128,512]{2,1,0:T(8,128)}, u32[]{:S(2)}) copy-start(f32[1,128,512]{2,1,0:T(8,128)} %param.20) | copy-start | bytes 786436
  89.1 161.5 %copy-start.15 = (bf16[1,128,512]{1,2,0:T(8,128)(2,1)}, bf16[1,128,512]{1,2,0:T(8,128)(2,1)S(1)}, u32[]{:S(2)}) copy-start(bf16[1,128,512]{1,2,0:T(8,128)(2,1)S(1)} %copy.198) | copy-start | bytes 393220
  94.4 2.7 copy-start.8
  121.1 5.2 copy-start.9
  141.5 5.5 copy-start.27
  148.7 14.4 %copy-start.25 = (f32[1,31,512]{1,2,0:T(8,128)S(1)}, f32[1,31,512]{1,2,0:T(8,128)}, u32[]{:S(2)}) copy-start(f32[1,31,512]{1,2,0:T(8,128)} %get-tuple-element.1003) | copy-start | bytes 190468
  153.3 12.2 %copy-start.34 = (f32[1,1,512]{2,1,0:T(1,128)S(1)}, f32[1,1,512]{2,1,0:T(1,128)}, u32[]{:S(2)}) copy-start(f32[1,1,512]{2,1,0:T(1,128)} %slice.490) | copy-start | bytes 6148
  165.6 5.6 copy-start.10
  165.7 10.5 %copy-start.33 = (f32[1,1,512]{2,1,0:T(1,128)S(1)}, f32[1,1,512]{2,1,0:T(1,128)}, u32[]{:S(2)}) copy-start(f32[1,1,512]{2,1,0:T(1,128)} %slice.439) | copy-start | bytes 6148
  176.3 75.3 %copy-start.31 = (bf16[1,128,512]{2,1,0:T(8,128)(2,1)S(1)}, bf16[1,128,512]{2,1,0:T(8,128)(2,1)}, u32[]{:S(2)}) copy-start(bf16[1,128,512]{2,1,0:T(8,128)(2,1)} %param.17) | copy-start | bytes 393220
  176.4 76.0 %copy-start.19 = (bf16[1,128,1024]{2,1,0:T(8,128)(2,1)S(1)}, bf16[1,128,1024]{2,1,0:T(8,128)(2,1)}, u32[]{:S(2)}) copy-start(bf16[1,128,1024]{2,1,0:T(8,128)(2,1)} %param.22) | copy-start | bytes 786436
  249.3 5.9 copy-start.14
  251.5 175.5 %all-gather.10.cloned.1.call-start = ((), (), s32[]{:S(2)}) async-start(), calls=%async_computation.3 | async-start | bytes 4325376 | tf_op jit(solution)/shard_map/all_gather | solution.py:162
  252.4 210.7 %all-gather.12.cloned.1.call-start = ((), (), s32[]{:S(2)}) async-start(), calls=%async_computation.4 | async-start | bytes 4325376 | tf_op jit(solution)/shard_map/all_gather | solution.py:163
  255.3 24.0 %copy-start.3 = (bf16[1,128,512]{1,2,0:T(8,128)(2,1)S(1)}, bf16[1,128,512]{1,2,0:T(8,128)(2,1)}, u32[]{:S(2)}) copy-start(bf16[1,128,512]{1,2,0:T(8,128)(2,1)} %copy.200) | copy-start | bytes 393220
  322.5 1.3 copy-start.7
  327.9 2.2 copy-start.7
  335.3 2.2 copy-start.7
  342.6 2.2 copy-start.7
  350.0 2.2 copy-start.7
  357.3 2.2 copy-start.7
  364.7 2.2 copy-start.7
  372.0 2.2 copy-start.7
  380.0 83.0 %all-to-all-start = ((f32[32,1,128,8]{2,3,1,0:T(8,128)}), f32[32,1,128,8]{2,3,1,0:T(8,128)}, u32[]{:S(2)}, u32[]{:S(2)}) async-start(f32[32,1,128,8]{2,3,1,0:T(8,128)} %stack.2), calls=%async_computation | async-start | bytes 262144 | tf_op jit(solution)/shard_map/all_to_all | solution.py:152
  385.9 349.7 %all-reduce.61.cloned.1.call-start = ((), (), s32[]{:S(2)}) async-start(), calls=%async_computation.5 | async-start | bytes 4194304
  387.0 76.1 %copy-start.4 = (f32[1,128,8,64]{1,3,2,0:T(8,128)S(1)}, f32[1,128,8,64]{1,3,2,0:T(8,128)}, u32[]{:S(2)}) copy-start(f32[1,128,8,64]{1,3,2,0:T(8,128)} %custom-call.8) | copy-start | bytes 786436
  387.0 76.1 %copy-start.6 = (bf16[1,128,512]{1,2,0:T(8,128)(2,1)S(1)}, bf16[1,128,512]{1,2,0:T(8,128)(2,1)}, u32[]{:S(2)}) copy-start(bf16[1,128,512]{1,2,0:T(8,128)(2,1)} %copy.199) | copy-start | bytes 393220
  464.3 0.8 copy-start.2
  534.2 14.5 %copy-start.23 = (f32[1,64,512]{1,2,0:T(8,128)S(1)}, f32[1,64,512]{1,2,0:T(8,128)}, u32[]{:S(2)}) copy-start(f32[1,64,512]{1,2,0:T(8,128)} %slice.510) | copy-start | bytes 393220
  534.3 14.5 %copy-start.24 = (f32[1,64,512]{1,2,0:T(8,128)S(1)}, f32[1,64,512]{1,2,0:T(8,128)}, u32[]{:S(2)}) copy-start(f32[1,64,512]{1,2,0:T(8,128)} %slice.517) | copy-start | bytes 393220
  593.7 22.6 %copy-start.16 = (f32[1,2,512]{1,2,0:T(8,128)S(1)}, f32[1,2,512]{1,2,0:T(8,128)}, u32[]{:S(2)}) copy-start(f32[1,2,512]{1,2,0:T(8,128)} %pad_add_fusion) | copy-start | bytes 12292
  624.0 2.7 copy-start.18
  629.5 1.4 copy-start.21
  635.5 4.7 copy-start.28
  635.5 4.7 copy-start.29
  640.2 2.7 copy-start.20
  642.9 5.0 copy-start.26
  645.6 2.4 copy-start.17
  648.0 18.0 %copy-start.11 = (f32[1,1,512]{1,2,0:T(8,128)S(1)}, f32[1,1,512]{1,2,0:T(8,128)}, u32[]{:S(2)}) copy-start(f32[1,1,512]{1,2,0:T(8,128)} %copy-done.10) | copy-start | bytes 6148
  656.8 73.0 %copy-start.32 = (f32[1,512]{1,0:T(1,128)S(1)}, f32[1,512]{1,0:T(1,128)}, u32[]{:S(2)}) copy-start(f32[1,512]{1,0:T(1,128)} %custom-call.9) | copy-start | bytes 6148
  666.0 65.4 %copy-start.30 = (f32[1,128,8,64]{1,3,2,0:T(8,128)S(1)}, f32[1,128,8,64]{1,3,2,0:T(8,128)}, u32[]{:S(2)}) copy-start(f32[1,128,8,64]{1,3,2,0:T(8,128)} %get-tuple-element.660) | copy-start | bytes 786436
  666.3 66.6 %copy-start.12 = (f32[1,128,512]{1,2,0:T(8,128)S(1)}, f32[1,128,512]{1,2,0:T(8,128)}, u32[]{:S(2)}) copy-start(f32[1,128,512]{1,2,0:T(8,128)} %get-tuple-element.957) | copy-start | bytes 786436
  666.3 66.6 %copy-start.22 = (f32[1,1,512]{1,2,0:T(8,128)S(1)}, f32[1,1,512]{1,2,0:T(8,128)}, u32[]{:S(2)}) copy-start(f32[1,1,512]{1,2,0:T(8,128)} %copy.220) | copy-start | bytes 6148
  732.2 5.2 copy-start.1
  (7 other events, 5.7 us)
Sparse Core Ops, SparseCore 0:
  9.8 75.0 all-gather.7
  251.6 68.9 all-gather.5
  323.0 71.5 all-gather.9
  396.3 66.6 all-gather.11
  468.3 263.9 all-reduce.60
